TPU v7x, 128 devices: a whole 4x4x4 slice. The times are simulated.
128 devices in a mesh: lm: 8 (over z, x_hi), sl: 16 (over y, x_lo, core).
Axes of the slice: x: 4 (x_hi: 2, x_lo: 2; x = x_hi * 2 + x_lo), y: 4, z: 4, core: 2. Of those that a mesh axis runs over, the one named last changes fastest.
Arguments:
- slab: bfloat16 [16384, 1024], P('sl'), may hold values from -6 to 6
- landmarks: bfloat16 [32768, 1024], P(('lm', 'sl')), may hold values from -6 to 6
- codes: bfloat16 [32768, 96], P(('lm', 'sl')), may hold values from -4 to 4
- exponents: int32 [256], P(('lm', 'sl')), may hold values from -3 to 3
- eigvec: bfloat16 [96, 64], replicated, may hold values from -0.625 to 0.625
- ritz: float32 [64], replicated, may hold values from 0.5 to 4
Outputs:
- extended: float32 [16384, 64], P('sl')
All inputs are finite; a program needn't handle non-finite values.
Results may differ from a plain program's by a relative error of at most 0.004.
Values may be sent and summed in bfloat16 or wider, within the bound.
A program may use at most 128 MiB of HBM per device.

v0:
```python
import math

import jax
import jax.numpy as jnp
from jax import lax
from jax.sharding import PartitionSpec as P

BLOCK = 128


def affinity_sum(rows, land_piece, vec_piece, coeff):
    scores = jnp.dot(rows, land_piece.T, preferred_element_type=jnp.float32) * coeff
    affinity = jnp.exp(scores).astype(jnp.bfloat16)
    return jnp.dot(affinity, vec_piece, preferred_element_type=jnp.float32)


def local(slab, landmarks, codes, exponents, eigvec, ritz):
    total_land = codes.shape[0] * lax.axis_size("lm") * lax.axis_size("sl")
    coeff = 1.0 / math.sqrt(slab.shape[1])
    factor = 1.0 / (ritz * math.sqrt(total_land))
    scale = jnp.exp2(exponents.astype(jnp.float32))
    rows_scale = jnp.repeat(scale, BLOCK)
    basis = (codes.astype(jnp.float32) * rows_scale[:, None]).astype(jnp.bfloat16)
    vectors = jnp.dot(basis, eigvec, preferred_element_type=jnp.float32).astype(jnp.bfloat16)
    terms = affinity_sum(lax.all_gather(slab, "sl", axis=0, tiled=True), landmarks, vectors, coeff)
    partial_sum = lax.psum_scatter(terms, "sl", scatter_dimension=0, tiled=True)
    summed = lax.psum(partial_sum, "lm")
    return summed * factor[None, :]


def solution(mesh):
    return jax.shard_map(
        local,
        mesh=mesh,
        in_specs=(
            P("sl", None),
            P(("lm", "sl"), None),
            P(("lm", "sl"), None),
            P(("lm", "sl")),
            P(),
            P(),
        ),
        out_specs=P("sl", None),
        check_vma=False,
    )
```

profile of v0, /device:TPU:0, one launch (start us, length us, event | category | flops | bytes accessed | tf_op | source)
XLA Modules:
  0.0 365.8 jit_solution(13882836581902991858)
XLA Ops:
  6.5 0.0 copy-start
  6.5 0.0 all-gather.2.cloned.1.call-start
  6.5 0.7 all-gather.2.cloned.1.call-update
  7.3 0.0 reduce-scatter.2.cloned.1.call-start
  7.3 0.7 multiply_exponential_fusion
  8.0 0.1 broadcast_bitcast_fusion
  8.0 1.0 convolution_convert_fusion
  9.0 0.0 copy-start.1
  9.0 173.1 %all-gather.2.cloned.1.call-done = bf16[16384,1024]{1,0:T(8,128)(2,1)} async-done(((bf16[1024,1024]{1,0:T(8,128)(2,1)}), bf16[16384,1024]{1,0:T(8,128)(2,1)}) %all-gather.2.cloned.1.call-update) | async-done | bytes 33554448 | tf_op jit(solution)/shard_map/all_gather | solution.py:25
  182.1 0.0 copy-done
  182.1 18.8 %fusion.2 = f32[16384,64]{0,1:T(8,128)} fusion(bf16[256,64]{1,0:T(8,128)(2,1)S(1)} %convolution_convert_fusion, bf16[16384,1024]{1,0:T(8,128)(2,1)} %all-gather.2.cloned.1.call-done, bf16[256,1024]{1,0:T(8,128)(2,1)S(1)} %copy-done), kind=kOutput, calls=%fused_computation.3 | convolution fusion | flops 9135194112 | bytes 38305792 | tf_op jit(solution)/shard_map/dot_general | solution.py:14
  201.0 0.0 reduce-scatter.2.cloned.1.call-update
  201.0 0.0 all-reduce.2.cloned.1.call-start
  201.1 70.5 %reduce-scatter.2.cloned.1.call-done = f32[1024,64]{0,1:T(8,128)} async-done(((f32[16384,64]{0,1:T(8,128)}), f32[1024,64]{0,1:T(8,128)}) %reduce-scatter.2.cloned.1.call-update) | async-done | bytes 262160 | tf_op jit(solution)/shard_map/reduce_scatter | solution.py:26
  271.5 0.0 all-reduce.2.cloned.1.call-update
  271.6 0.0 copy-done.1
  271.6 85.9 %all-reduce.2.cloned.1.call-done = f32[1024,64]{0,1:T(8,128)} async-done(((f32[1024,64]{0,1:T(8,128)}), f32[1024,64]{0,1:T(8,128)}) %all-reduce.2.cloned.1.call-update) | async-done | bytes 262160 | tf_op jit(solution)/shard_map/psum | solution.py:27
  357.5 1.7 broadcast_multiply_fusion
  (1 shorter events, 0.0 us)
Async XLA Ops:
  6.5 175.6 %copy-start = (bf16[256,1024]{1,0:T(8,128)(2,1)S(1)}, bf16[256,1024]{1,0:T(8,128)(2,1)}, u32[]{:S(2)}) copy-start(bf16[256,1024]{1,0:T(8,128)(2,1)} %param.7) | copy-start | bytes 1572868
  6.5 175.6 %all-gather.2.cloned.1.call-start = ((), (), s32[]{:S(2)}) async-start(), calls=%async_computation.1 | async-start | bytes 35651584 | tf_op jit(solution)/shard_map/all_gather | solution.py:25
  7.3 264.3 %reduce-scatter.2.cloned.1.call-start = ((), (), s32[]{:S(2)}) async-start(), calls=%async_computation.2 | async-start | bytes 4456448 | tf_op jit(solution)/shard_map/reduce_scatter | solution.py:26
  9.0 262.5 %copy-start.1 = (f32[64]{0:T(128)S(1)}, f32[64]{0:T(128)}, u32[]{:S(2)}) copy-start(f32[64]{0:T(128)} %param.11) | copy-start | bytes 772
  201.0 156.5 %all-reduce.2.cloned.1.call-start = ((), (), s32[]{:S(2)}) async-start(), calls=%async_computation.3 | async-start | bytes 524288 | tf_op jit(solution)/shard_map/psum | solution.py:27
Sparse Core Ops, SparseCore 0:
  9.1 173.0 all-gather.1
  201.1 70.3 reduce-scatter.1
  274.0 83.4 all-reduce.1
where the time goes:
time: 366 us
  waiting for transfers between devices  330 us (90%)
  matrix products  19.8 us (5%)
  between operations  13.1 us (4%)
    all_gather x1, waiting for transfers between devices, local(): lax.all_gather(slab, 'sl', axis=0, tiled=True)  173 us
    psum x1, waiting for transfers between devices, local(): summed = lax.psum(partial_sum, 'lm')  85.9 us
    reduce_scatter x1, waiting for transfers between devices, local(): partial_sum = lax.psum_scatter(terms, 'sl', scatter_dimension=0, tiled=True)  70.5 us
    dot_general x1, matrix products, affinity_sum(): return jnp.dot(affinity, vec_piece, preferred_element_type=jnp.float32)  18.8 us
  transfers between devices with their start and end apart: 3, of which 3 were waited for; matrix products, arithmetic and copies ran while one was open for 0% of the time, Pallas kernels for 0%

commit v1 on v0

v1 whole, which is shorter than its diff:
```python
import math

import jax
import jax.numpy as jnp
from jax import lax
from jax.sharding import PartitionSpec as P

BLOCK = 128


def local(slab, landmarks, codes, exponents, eigvec, ritz):
    total_land = codes.shape[0] * lax.axis_size("lm") * lax.axis_size("sl")
    coeff = 1.0 / math.sqrt(slab.shape[1])
    factor = 1.0 / (ritz * math.sqrt(total_land))
    scale = jnp.exp2(exponents.astype(jnp.float32))
    rows_scale = jnp.repeat(scale, BLOCK)
    basis = (codes.astype(jnp.float32) * rows_scale[:, None]).astype(jnp.bfloat16)
    vectors = jnp.dot(basis, eigvec, preferred_element_type=jnp.float32).astype(jnp.bfloat16)
    land = lax.all_gather(landmarks, "sl", axis=0, tiled=True)
    vec = lax.all_gather(vectors, "sl", axis=0, tiled=True)
    scores = jnp.dot(slab, land.T, preferred_element_type=jnp.float32) * coeff
    affinity = jnp.exp(scores).astype(jnp.bfloat16)
    terms = jnp.dot(affinity, vec, preferred_element_type=jnp.float32)
    summed = lax.psum(terms, "lm")
    return summed * factor[None, :]


def solution(mesh):
    return jax.shard_map(
        local,
        mesh=mesh,
        in_specs=(
            P("sl", None),
            P(("lm", "sl"), None),
            P(("lm", "sl"), None),
            P(("lm", "sl")),
            P(),
            P(),
        ),
        out_specs=P("sl", None),
        check_vma=False,
    )
```

time: 366 us -> 178 us (0.49)
  waiting for transfers between devices: 330 us -> 116 us
  blocking collectives: 0 us -> 30 us
    all_gather x1, waiting for transfers between devices: 173 us -> 27.3 us  [local(): land = lax.all_gather(landmarks, 'sl', axis=0, tiled=True)]
    reduce_scatter x1 -> x0, waiting for transfers between devices: 70.5 us -> none  [local(): partial_sum = lax.psum_scatter(terms, 'sl', scatter_dimension=0, tiled=True)]
    all_gather x0 -> x1, blocking collectives: none -> 30 us  [local(): vec = lax.all_gather(vectors, 'sl', axis=0, tiled=True)]
  transfers between devices with their start and end apart: 3 -> 2, of which waited for: 3 -> 2; matrix products, arithmetic and copies ran while one was open for 0% -> 1% of each run, Pallas kernels for 0% -> 0%
where the time goes in v1:
time: 178 us
  waiting for transfers between devices  116 us (65%)
  blocking collectives  30 us (17%)
  matrix products  16.6 us (9%)
  between operations  13.4 us (8%)
  other arithmetic  2.4 us (1%)
    psum x1, waiting for transfers between devices, local(): summed = lax.psum(terms, 'lm')  87.6 us
    all_gather x1, blocking collectives, local(): vec = lax.all_gather(vectors, 'sl', axis=0, tiled=True)  30 us
    all_gather x1, waiting for transfers between devices, local(): land = lax.all_gather(landmarks, 'sl', axis=0, tiled=True)  27.3 us
    dot_general x1, matrix products, local(): terms = jnp.dot(affinity, vec, preferred_element_type=jnp.float32)  15.6 us
  transfers between devices with their start and end apart: 2, of which 2 were waited for; matrix products, arithmetic and copies ran while one was open for 1% of the time, Pallas kernels for 0%

profile of v1, /device:TPU:0, one launch (start us, length us, event | category | flops | bytes accessed | tf_op | source)
XLA Modules:
  0.0 178.2 jit_solution(8846013648305641239)
XLA Ops:
  6.5 0.0 copy-start
  6.5 0.0 all-gather.2.cloned.1.call-start
  6.5 0.7 all-gather.2.cloned.1.call-update
  7.3 0.0 all-reduce.2.cloned.1.call-start
  7.3 0.7 multiply_exponential_fusion
  8.0 0.1 broadcast_bitcast_fusion
  8.0 1.0 convolution_convert_fusion
  9.0 30.0 %all_gather.7 = bf16[4096,64]{1,0:T(8,128)(2,1)S(1)} all-gather(bf16[256,64]{1,0:T(8,128)(2,1)S(1)} %convolution_convert_fusion), channel_id=1, replica_groups=mesh['lm'=8,'sl'=16] {'sl'}, dimensions={0}, use_global_device_ids=true | all-gather | bytes 557056 | tf_op jit(solution)/shard_map/all_gather | solution.py:20
  39.1 0.0 copy-start.1
  39.1 27.3 %all-gather.2.cloned.1.call-done = bf16[4096,1024]{1,0:T(8,128)(2,1)} async-done(((bf16[256,1024]{1,0:T(8,128)(2,1)}), bf16[4096,1024]{1,0:T(8,128)(2,1)}) %all-gather.2.cloned.1.call-update) | async-done | bytes 8388624 | tf_op jit(solution)/shard_map/all_gather | solution.py:19
  66.4 0.0 copy-done
  66.4 15.6 %fusion.1 = f32[1024,64]{0,1:T(8,128)} fusion(bf16[4096,64]{1,0:T(8,128)(2,1)S(1)} %all_gather.7, bf16[1024,1024]{1,0:T(8,128)(2,1)S(1)} %copy-done, bf16[4096,1024]{1,0:T(8,128)(2,1)} %all-gather.2.cloned.1.call-done), kind=kOutput, calls=%fused_computation.8 | convolution fusion | flops 9135194112 | bytes 11272192 | tf_op jit(solution)/shard_map/dot_general | solution.py:23
  82.0 0.0 all-reduce.2.cloned.1.call-update
  82.0 0.0 copy-done.1
  82.0 87.6 %all-reduce.2.cloned.1.call-done = f32[1024,64]{0,1:T(8,128)} async-done(((f32[1024,64]{0,1:T(8,128)}), f32[1024,64]{0,1:T(8,128)}) %all-reduce.2.cloned.1.call-update) | async-done | bytes 262160 | tf_op jit(solution)/shard_map/psum | solution.py:24
  169.6 1.7 broadcast_multiply_fusion
  (1 shorter events, 0.0 us)
Async XLA Ops:
  6.5 59.8 %copy-start = (bf16[1024,1024]{1,0:T(8,128)(2,1)S(1)}, bf16[1024,1024]{1,0:T(8,128)(2,1)}, u32[]{:S(2)}) copy-start(bf16[1024,1024]{1,0:T(8,128)(2,1)} %param.6) | copy-start | bytes 6291460
  6.5 59.8 %all-gather.2.cloned.1.call-start = ((), (), s32[]{:S(2)}) async-start(), calls=%async_computation | async-start | bytes 8912896 | tf_op jit(solution)/shard_map/all_gather | solution.py:19
  7.3 162.3 %all-reduce.2.cloned.1.call-start = ((), (), s32[]{:S(2)}) async-start(), calls=%async_computation.1 | async-start | bytes 524288 | tf_op jit(solution)/shard_map/psum | solution.py:24
  39.1 42.9 %copy-start.1 = (f32[64]{0:T(128)S(1)}, f32[64]{0:T(128)}, u32[]{:S(2)}) copy-start(f32[64]{0:T(128)} %param.11) | copy-start | bytes 772
Sparse Core Ops, SparseCore 0:
  9.1 57.2 all-gather.1
  82.1 87.4 all-reduce.1

commit v2 on v1

v2 whole, which is shorter than its diff:
```python
import functools
import math

import jax
import jax.numpy as jnp
from jax import lax
from jax.experimental import pallas as pl
from jax.experimental.pallas import tpu as pltpu
from jax.sharding import PartitionSpec as P

MESH = pl.DeviceIdType.MESH
HALVES = 2
QUARTERS = 4
GROUPS = 8
NT = (((1,), (1,)), ((), ()))
NN = (((1,), (0,)), ((), ()))


def group_of(col, rel, half):
    if rel == 0:
        return col
    if rel == 2:
        return 6 + col
    early = (rel == -1) == (half == 0)
    return (2 if early else 3) + 2 * col


def kernel(
    slab_hbm, land_hbm, codes_ref, exponents_ref, eigvec_ref, out_ref,
    slab, land, vec, acc, swap_out, swap_in, total, rs_out, rs_in, ag_in,
    load_sem, slab_sem, own_send, fwd_send, vec_send, land_recv, vec_recv, swap_sem, rs_send, rs_recv, ag_send, ag_recv,
):
    rows = slab_hbm.shape[0]
    width = land_hbm.shape[0]
    quarter = width // QUARTERS
    n_lm = lax.axis_size("lm")
    chunk = rows // n_lm
    scale = math.log2(math.e) / math.sqrt(slab_hbm.shape[1])

    lm = lax.axis_index("lm")
    sl = lax.axis_index("sl")
    z, x_hi = lm // 2, lm % 2
    y, x_lo, core = sl // 4, (sl // 2) % 2, sl % 2
    x = x_hi * 2 + x_lo
    side = 1 - 2 * core

    def place(dx, dy, flip=0):
        px = lax.rem(x + dx + 4, 4)
        py = lax.rem(y + dy + 4, 4)
        pc = lax.rem(core + flip, 2)
        return (z * 2 + px // 2, py * 4 + lax.rem(px, 2) * 2 + pc)

    def peer(r):
        return (lax.rem(lm + r, n_lm), sl)

    up, down, across, partner = place(0, 1), place(0, -1), place(side, 0), place(0, 0, 1)

    load_slab = pltpu.make_async_copy(slab_hbm, slab.at[0], load_sem.at[0])
    load_land = pltpu.make_async_copy(land_hbm, land.at[0], load_sem.at[1])
    load_slab.start()
    load_land.start()

    barrier = pltpu.get_barrier_semaphore()
    greeted = [place(0, 1), place(0, -1), place(0, 2), partner]
    greeted += [place(d * side, dy) for d in (1, -1) for dy in (0, 1, -1, 2)]
    greeted += [peer(r) for r in range(1, n_lm)]
    for device in greeted:
        pl.semaphore_signal(barrier, inc=1, device_id=device, device_id_type=MESH)

    block = codes_ref.shape[1] // exponents_ref.shape[0]
    for half in range(HALVES):
        grow = jnp.exp2(jnp.full((codes_ref.shape[0], block), exponents_ref[half], jnp.int32).astype(jnp.float32))
        basis = (codes_ref[:, half * block:(half + 1) * block].astype(jnp.float32) * grow).astype(jnp.bfloat16)
        vec[0, half] = lax.dot_general(eigvec_ref[...], basis, NN, preferred_element_type=jnp.float32).astype(jnp.bfloat16)

    pl.semaphore_wait(barrier, len(greeted))

    def remote(src, dst, send, recv, device):
        return pltpu.make_async_remote_copy(
            src_ref=src, dst_ref=dst, send_sem=send, recv_sem=recv, device_id=device, device_id_type=MESH
        )

    sent = []

    def start(copy):
        copy.start()
        sent.append(copy)

    def quarter_of(g, q):
        return land.at[g, pl.ds(q * quarter, quarter)]

    def own(q, g, device, sem):
        start(remote(land_hbm.at[pl.ds(q * quarter, quarter)], quarter_of(g, q), own_send.at[sem], land_recv.at[g, q], device))

    for i in range(QUARTERS):
        own(i, group_of(1, 0, i // 2), across, 3 * i)
        own(i, group_of(0, -1, i // 2), up, 3 * i + 1)
        j = (i + 2) % QUARTERS
        own(j, group_of(0, 1, j // 2), down, 3 * i + 2)

    swap_slab = remote(slab_hbm, slab.at[1], slab_sem.at[0], slab_sem.at[1], partner)
    swap_slab.start()

    n_vec = 0
    for col in (0, 1):
        for rel, dy in ((0, 0), (-1, 1), (1, -1), (2, 2)):
            if col == 0 and rel == 0:
                continue
            for half in range(HALVES):
                g = group_of(col, rel, half)
                start(remote(vec.at[0, half], vec.at[g, half], vec_send.at[n_vec], vec_recv, place(col * side, dy)))
                n_vec += 1

    n_fwd = [0]

    def arrive(g, q):
        remote(quarter_of(g, q), quarter_of(g, q), fwd_send.at[0], land_recv.at[g, q], partner).wait_recv()

    def forward(g, q, to_g, device):
        start(remote(quarter_of(g, q), quarter_of(to_g, q), fwd_send.at[n_fwd[0]], land_recv.at[to_g, q], device))
        n_fwd[0] += 1

    def multiply(g, side_of, first=False):
        scores = lax.dot_general(land[g], slab[side_of], NT, preferred_element_type=jnp.float32)
        affinity = jnp.exp2(scores * scale).astype(jnp.bfloat16)
        coeffs = jnp.concatenate([vec[g, 0], vec[g, 1]], axis=1)
        part = lax.dot_general(coeffs, affinity, NN, preferred_element_type=jnp.float32)
        acc[side_of] = part if first else acc[side_of] + part

    load_slab.wait()
    load_land.wait()
    multiply(0, 0, first=True)
    swap_slab.wait_recv()
    multiply(0, 1, first=True)

    for q0, q1 in ((0, 2), (1, 3)):
        arrive(2, q0)
        forward(2, q0, group_of(1, -1, 0), across)
        forward(2, q0, 6, up)
        arrive(2, q1)
        forward(2, q1, group_of(1, 1, 1), across)
        forward(2, q1, 6, down)
    remote(vec.at[pl.ds(1, GROUPS - 1)], vec.at[pl.ds(1, GROUPS - 1)], fwd_send.at[0], vec_recv, partner).wait_recv()
    for q in range(QUARTERS):
        arrive(1, q)
    for g in (2, 1):
        for s in (0, 1):
            multiply(g, s)

    for q0, q1 in ((0, 2), (1, 3)):
        arrive(3, q1)
        forward(3, q1, group_of(1, -1, 1), across)
        arrive(3, q0)
        forward(3, q0, group_of(1, 1, 0), across)
    for q in (0, 2, 1, 3):
        arrive(4, q)
    forward(4, 1, 7, up)
    forward(4, 3, 7, down)
    for g in (3, 4):
        for s in (0, 1):
            multiply(g, s)

    for q in (0, 2):
        arrive(6, q)
        forward(6, q, 7, across)
    for q in (2, 0, 3, 1):
        arrive(5, q)
    for s in (0, 1):
        multiply(5, s)
    for q in (1, 3):
        arrive(6, q)
    for s in (0, 1):
        multiply(6, s)

    for q in range(QUARTERS):
        arrive(7, q)
    multiply(7, 1)
    swap_out[...] = acc[1].astype(swap_out.dtype)
    swap = remote(swap_out, swap_in, swap_sem.at[0], swap_sem.at[1], partner)
    swap.start()
    multiply(7, 0)
    swap.wait_recv()
    for j in range(n_lm):
        lanes = slice(j * chunk, (j + 1) * chunk)
        piece = acc[0, :, lanes] + swap_in[:, lanes].astype(jnp.float32)
        total[j] = piece
        rs_out[j] = piece.astype(rs_out.dtype)
    for r in (5, 3, 4, 2, 6, 1, 7):
        j = lax.rem(lm + r, n_lm)
        start(remote(rs_out.at[j], rs_in.at[r - 1], rs_send.at[r - 1], rs_recv, peer(r)))
    remote(rs_in, rs_in, fwd_send.at[0], rs_recv, partner).wait_recv()
    piece = total[lm]
    for r in range(n_lm - 1):
        piece = piece + rs_in[r].astype(jnp.float32)
    ag_in[lm] = piece.astype(ag_in.dtype)
    gathered = []
    for r in (5, 3, 4, 2, 6, 1, 7):
        copy = remote(ag_in.at[lm], ag_in.at[lm], ag_send.at[r - 1], ag_recv.at[r - 1], peer(r))
        copy.start()
        gathered.append(copy)
    for copy in gathered:
        copy.wait_recv()
    for j in range(n_lm):
        out_ref[:, j * chunk:(j + 1) * chunk] = ag_in[j].astype(out_ref.dtype)

    for copy in sent + gathered + [swap_slab, swap]:
        copy.wait_send()


def local(slab, landmarks, codes, exponents, eigvec, ritz):
    n_lm, n_sl = lax.axis_size("lm"), lax.axis_size("sl")
    total_land = codes.shape[0] * n_lm * n_sl
    rows, feat = slab.shape
    width = landmarks.shape[0]
    ritz_n = eigvec.shape[1]
    block = codes.shape[0] // exponents.shape[0]
    chunk = rows // n_lm
    wire = jnp.bfloat16
    summed = pl.pallas_call(
        kernel,
        out_shape=jax.ShapeDtypeStruct((ritz_n, rows), jnp.float32),
        in_specs=[
            pl.BlockSpec(memory_space=pl.ANY),
            pl.BlockSpec(memory_space=pl.ANY),
            pl.BlockSpec(memory_space=pltpu.VMEM),
            pl.BlockSpec(memory_space=pltpu.SMEM),
            pl.BlockSpec(memory_space=pltpu.VMEM),
        ],
        out_specs=pl.BlockSpec(memory_space=pltpu.VMEM),
        scratch_shapes=[
            pltpu.VMEM((2, rows, feat), slab.dtype),
            pltpu.VMEM((GROUPS, width, feat), landmarks.dtype),
            pltpu.VMEM((GROUPS, HALVES, ritz_n, block), jnp.bfloat16),
            pltpu.VMEM((2, ritz_n, rows), jnp.float32),
            pltpu.VMEM((ritz_n, rows), wire),
            pltpu.VMEM((ritz_n, rows), wire),
            pltpu.VMEM((n_lm, ritz_n, chunk), jnp.float32),
            pltpu.VMEM((n_lm, ritz_n, chunk), wire),
            pltpu.VMEM((n_lm - 1, ritz_n, chunk), wire),
            pltpu.VMEM((n_lm, ritz_n, chunk), wire),
            pltpu.SemaphoreType.DMA((2,)),
            pltpu.SemaphoreType.DMA((2,)),
            pltpu.SemaphoreType.DMA((3 * QUARTERS,)),
            pltpu.SemaphoreType.DMA((16,)),
            pltpu.SemaphoreType.DMA((14,)),
            pltpu.SemaphoreType.DMA((GROUPS, QUARTERS)),
            pltpu.SemaphoreType.DMA,
            pltpu.SemaphoreType.DMA((2,)),
            pltpu.SemaphoreType.DMA((n_lm - 1,)),
            pltpu.SemaphoreType.DMA,
            pltpu.SemaphoreType.DMA((n_lm - 1,)),
            pltpu.SemaphoreType.DMA((n_lm - 1,)),
        ],
        compiler_params=pltpu.CompilerParams(collective_id=0, has_side_effects=True, vmem_limit_bytes=56 * 2**20),
        name="nystrom",
    )(slab, landmarks, codes.T, exponents, eigvec.T)
    factor = 1.0 / (ritz * math.sqrt(total_land))
    return (summed * factor[:, None]).T


def solution(mesh):
    return jax.shard_map(
        local,
        mesh=mesh,
        in_specs=(
            P("sl", None),
            P(("lm", "sl"), None),
            P(("lm", "sl"), None),
            P(("lm", "sl")),
            P(),
            P(),
        ),
        out_specs=P("sl", None),
        check_vma=False,
    )
```

time: 178 us -> 57.7 us (0.32)
  waiting for transfers between devices: 116 us -> 0 us
  Pallas kernels: 0 us -> 55.1 us
  blocking collectives: 30 us -> 0 us
  matrix products: 16.6 us -> 0 us
  between operations: 13.4 us -> 0.01 us
    psum x1 -> x0, waiting for transfers between devices: 87.6 us -> none  [local(): summed = lax.psum(terms, 'lm')]
    pallas_call x0 -> x1, Pallas kernels: none -> 55.1 us  [local(): pl.pallas_call(kernel, out_shape=jax.ShapeDtypeStruct((ritz_n, rows), jnp...]
    all_gather x1 -> x0, blocking collectives: 30 us -> none  [local(): vec = lax.all_gather(vectors, 'sl', axis=0, tiled=True)]
    all_gather x1 -> x0, waiting for transfers between devices: 27.3 us -> none  [local(): land = lax.all_gather(landmarks, 'sl', axis=0, tiled=True)]
    dot_general x2 -> x0, matrix products: 16.6 us -> none  [the longest x1 15.6 us: local(): terms = jnp.dot(affinity, vec, preferred_element_type=jnp.float32)]
  transfers between devices with their start and end apart: 2 -> 0, of which waited for: 2 -> 0; matrix products, arithmetic and copies ran while one was open for 1% -> 0% of each run, Pallas kernels for 0% -> 0%
where the time goes in v2:
time: 57.7 us; the launch traced here: 57.5 us
  Pallas kernels  55.1 us (95%)
  other arithmetic  2.4 us (4%)
    pallas_call x1, Pallas kernels, local(): pl.pallas_call(kernel, out_shape=jax.ShapeDtypeStruct((ritz_n, rows), jnp...  55.1 us
    transpose x1, other arithmetic, local(): return (summed * factor[:, None]).T  1.74 us

profile of v2, /device:TPU:0, one launch (start us, length us, event | category | flops | bytes accessed | tf_op | source)
XLA Modules:
  0.0 57.5 jit_solution(2026492450628247352)
XLA Ops:
  0.0 0.7 %multiply_divide_fusion = f32[64]{0:T(128)S(1)} fusion(f32[64]{0:T(128)} %param.11), kind=kLoop, calls=%fused_computation.1 | loop fusion | flops 128 | bytes 512 | tf_op jit(solution)/shard_map/div | solution.py:257
  0.7 55.1 %nystrom.1 = f32[64,1024]{1,0:T(8,128)} custom-call(bf16[1024,1024]{1,0:T(8,128)(2,1)} %slab_hbm.1, bf16[256,1024]{1,0:T(8,128)(2,1)} %land_hbm.1, bf16[96,256]{1,0:T(8,128)(2,1)} %bitcast.4, s32[2]{0:T(128)} %exponents_ref.1, bf16[64,96]{1,0:T(8,128)(2,1)} %bitcast.5), custom_call_target="tpu_custom_call" | custom-call | tf_op jit(solution)/shard_map/nystrom/pallas_call | solution.py:219
  55.7 1.7 %multiply_bitcast_fusion = f32[1024,64]{0,1:T(8,128)} fusion(f32[64,1024]{1,0:T(8,128)} %nystrom.1, f32[64]{0:T(128)S(1)} %multiply_divide_fusion), kind=kLoop, calls=%fused_computation | loop fusion | flops 65536 | bytes 524544 | tf_op jit(solution)/shard_map/transpose | solution.py:258

commit v3 on v2

v3 whole, which is shorter than its diff:
```python
import functools
import math

import jax
import jax.numpy as jnp
from jax import lax
from jax.experimental import pallas as pl
from jax.experimental.pallas import tpu as pltpu
from jax.sharding import PartitionSpec as P

MESH = pl.DeviceIdType.MESH
HALVES = 2
QUARTERS = 4
GROUPS = 8
NT = (((1,), (1,)), ((), ()))
NN = (((1,), (0,)), ((), ()))


def group_of(col, rel, half):
    if rel == 0:
        return col
    if rel == 2:
        return 6 + col
    early = (rel == -1) == (half == 0)
    return (2 if early else 3) + 2 * col


def kernel(
    slab_hbm, land_hbm, codes_hbm, exponents_hbm, eigvec_hbm, ritz_hbm, out_ref,
    slab, land, vec, acc, swap_out, swap_in, total, rs_out, rs_in, ag_in, codes, exponents, eigvec, ritz,
    load_sem, slab_sem, own_send, fwd_send, vec_send, land_recv, vec_recv, swap_sem, rs_send, rs_recv, ag_send, ag_recv, near,
):
    rows, feat = slab_hbm.shape
    width = land_hbm.shape[0]
    quarter = width // QUARTERS
    n_lm, n_sl = lax.axis_size("lm"), lax.axis_size("sl")
    chunk = rows // n_lm
    scale = math.log2(math.e) / math.sqrt(feat)

    lm = lax.axis_index("lm")
    sl = lax.axis_index("sl")
    z, x_hi = lm // 2, lm % 2
    y, x_lo, core = sl // 4, (sl // 2) % 2, sl % 2
    x = x_hi * 2 + x_lo
    side = 1 - 2 * core

    def place(dx, dy, dz=0, flip=0):
        px = lax.rem(x + dx + 4, 4)
        py = lax.rem(y + dy + 4, 4)
        pz = lax.rem(z + dz + 4, 4)
        pc = lax.rem(core + flip, 2)
        return (pz * 2 + px // 2, py * 4 + lax.rem(px, 2) * 2 + pc)

    def peer(r):
        return (lax.rem(lm + r, n_lm), sl)

    up, down, across, partner = place(0, 1), place(0, -1), place(side, 0), place(0, 0, 0, 1)
    ring = [across, place(-side, 0), place(0, 0, 1), place(0, 0, -1)]

    def greet(semaphore, devices):
        for device in devices:
            pl.semaphore_signal(semaphore, inc=1, device_id=device, device_id_type=MESH)

    barrier = pltpu.get_barrier_semaphore()
    greeted = ring + [up, down, partner]
    greet(barrier, greeted)
    loads = [
        pltpu.make_async_copy(src, dst, load_sem.at[i])
        for i, (src, dst) in enumerate((
            (codes_hbm, codes), (eigvec_hbm, eigvec), (exponents_hbm, exponents), (ritz_hbm, ritz),
            (land_hbm, land.at[0]), (slab_hbm, slab.at[pl.ds(0, rows)]),
        ))
    ]
    for load in loads:
        load.start()
    pl.semaphore_wait(barrier, len(greeted))

    def remote(src, dst, send, recv, device):
        return pltpu.make_async_remote_copy(
            src_ref=src, dst_ref=dst, send_sem=send, recv_sem=recv, device_id=device, device_id_type=MESH
        )

    sent = []

    def start(copy):
        copy.start()
        sent.append(copy)

    def quarter_of(g, q):
        return land.at[g, pl.ds(q * quarter, quarter)]

    def own(i):
        for k, (col, rel, device) in enumerate(((1, 0, across), (0, -1, up), (0, 1, down))):
            q = (i + 2) % QUARTERS if rel == 1 else i
            g = group_of(col, rel, q // 2)
            src = land_hbm.at[pl.ds(q * quarter, quarter)]
            start(remote(src, quarter_of(g, q), own_send.at[3 * i + k], land_recv.at[g, q], device))

    n_vec = [0]

    def send_vec(g, half, to_g, device):
        start(remote(vec.at[g, half], vec.at[to_g, half], vec_send.at[n_vec[0]], vec_recv.at[to_g, half], device))
        n_vec[0] += 1

    def arrive_vec(g, half):
        remote(vec.at[g, half], vec.at[g, half], vec_send.at[0], vec_recv.at[g, half], partner).wait_recv()

    own(0)
    swap_slab = remote(slab_hbm, slab.at[pl.ds(rows, rows)], slab_sem.at[0], slab_sem.at[1], partner)
    swap_slab.start()
    for load in loads[:4]:
        load.wait()
    block = codes.shape[1] // HALVES
    for half in range(HALVES):
        grow = jnp.exp2(jnp.full((codes.shape[0], block), exponents[half], jnp.int32).astype(jnp.float32))
        basis = (codes[:, half * block:(half + 1) * block].astype(jnp.float32) * grow).astype(jnp.bfloat16)
        vec[0, half] = lax.dot_general(eigvec[...], basis, NN, preferred_element_type=jnp.float32).astype(jnp.bfloat16)
    for half in range(HALVES):
        for col, rel, device in ((0, -1, up), (0, 1, down), (1, 0, across)):
            send_vec(0, half, group_of(col, rel, half), device)
    for i in range(1, QUARTERS):
        own(i)
    greet(near.at[0], ring)

    n_fwd = [0]

    def arrive(g, q):
        remote(quarter_of(g, q), quarter_of(g, q), fwd_send.at[0], land_recv.at[g, q], partner).wait_recv()

    def forward(g, q, to_g, device):
        start(remote(quarter_of(g, q), quarter_of(to_g, q), fwd_send.at[n_fwd[0]], land_recv.at[to_g, q], device))
        n_fwd[0] += 1

    def multiply(g, n, lo, hi, first=False):
        part_of = slice(lo * rows, hi * rows)
        left = land[g:g + n].reshape(n * width, feat)
        scores = lax.dot_general(left, slab[part_of], NT, preferred_element_type=jnp.float32)
        affinity = jnp.exp2(scores * scale).astype(jnp.bfloat16)
        coeffs = jnp.concatenate([vec[g + i, half] for i in range(n) for half in range(HALVES)], axis=1)
        part = lax.dot_general(coeffs, affinity, NN, preferred_element_type=jnp.float32)
        acc[:, part_of] = part if first else acc[:, part_of] + part

    for load in loads[4:]:
        load.wait()
    multiply(0, 1, 0, 1, first=True)

    for g in (2, 3):
        for half in range(HALVES):
            arrive_vec(g, half)
            send_vec(g, half, g + 2, across)
            if g == 2:
                send_vec(g, half, 6, (up, down)[half])

    def step2(q0, q1):
        arrive(2, q0)
        forward(2, q0, 4, across)
        forward(2, q0, 6, up)
        arrive(2, q1)
        forward(2, q1, 4, across)
        forward(2, q1, 6, down)

    step2(0, 2)
    pl.semaphore_wait(near.at[0], len(ring))
    greet(near.at[1], ring)
    swap_slab.wait_recv()
    multiply(0, 1, 1, 2, first=True)
    step2(1, 3)
    for half in range(HALVES):
        arrive_vec(1, half)
    for q in range(QUARTERS):
        arrive(1, q)
    multiply(1, 2, 0, 2)

    for q0, q1 in ((0, 2), (1, 3)):
        arrive(3, q1)
        forward(3, q1, 5, across)
        arrive(3, q0)
        forward(3, q0, 5, across)
    pl.semaphore_wait(near.at[1], len(ring))
    greet(near.at[2], ring)
    for q in (0, 2, 1, 3):
        arrive(4, q)
    forward(4, 1, 7, up)
    forward(4, 3, 7, down)
    for half in range(HALVES):
        arrive_vec(6, half)
        send_vec(6, half, 7, across)
        arrive_vec(4, half)
    multiply(3, 2, 0, 2)

    for q in (0, 2):
        arrive(6, q)
        forward(6, q, 7, across)
    for half in range(HALVES):
        arrive_vec(5, half)
    for q in (2, 0, 3, 1):
        arrive(5, q)
    for q in (1, 3):
        arrive(6, q)
    multiply(5, 2, 0, 2)

    factor_row = 1.0 / (ritz[...] * math.sqrt(width * n_lm * n_sl))
    n_ritz = factor_row.shape[1]
    diagonal = lax.broadcasted_iota(jnp.int32, (n_ritz, n_ritz), 0) == lax.broadcasted_iota(jnp.int32, (n_ritz, n_ritz), 1)
    factor = jnp.sum(jnp.where(diagonal, factor_row, 0.0), axis=1, keepdims=True)

    for half in range(HALVES):
        arrive_vec(7, half)
    for q in (0, 2, 1, 3):
        arrive(7, q)
    multiply(7, 1, 1, 2)
    swap_out[...] = acc[:, rows:]
    swap = remote(swap_out, swap_in, swap_sem.at[0], swap_sem.at[1], partner)
    swap.start()
    multiply(7, 1, 0, 1)
    pl.semaphore_wait(near.at[2], len(ring))
    swap.wait_recv()
    for j in range(n_lm):
        lanes = slice(j * chunk, (j + 1) * chunk)
        piece = acc[:, lanes] + swap_in[:, lanes]
        total[j] = piece
        rs_out[j] = piece.astype(rs_out.dtype)
    for r in (5, 3, 4, 2, 6, 1, 7):
        j = lax.rem(lm + r, n_lm)
        start(remote(rs_out.at[j], rs_in.at[r - 1], rs_send.at[r - 1], rs_recv, peer(r)))
    remote(rs_in, rs_in, fwd_send.at[0], rs_recv, partner).wait_recv()
    piece = total[lm]
    for r in range(n_lm - 1):
        piece = piece + rs_in[r].astype(jnp.float32)
    ag_in[lm] = (piece * factor).astype(ag_in.dtype)
    gathered = []
    for r in (5, 3, 4, 2, 6, 1, 7):
        copy = remote(ag_in.at[lm], ag_in.at[lm], ag_send.at[r - 1], ag_recv.at[r - 1], peer(r))
        copy.start()
        gathered.append(copy)
    for copy in gathered:
        copy.wait_recv()
    for j in range(n_lm):
        out_ref[:, j * chunk:(j + 1) * chunk] = ag_in[j].astype(out_ref.dtype)

    for copy in sent + gathered + [swap_slab, swap]:
        copy.wait_send()


def local(slab, landmarks, codes, exponents, eigvec, ritz):
    n_lm = lax.axis_size("lm")
    rows, feat = slab.shape
    width = landmarks.shape[0]
    n_ritz = eigvec.shape[1]
    block = codes.shape[0] // exponents.shape[0]
    chunk = rows // n_lm
    wire = jnp.bfloat16
    dma = pltpu.SemaphoreType.DMA
    extended = pl.pallas_call(
        kernel,
        out_shape=jax.ShapeDtypeStruct((n_ritz, rows), jnp.float32),
        in_specs=[pl.BlockSpec(memory_space=pl.ANY)] * 6,
        out_specs=pl.BlockSpec(memory_space=pltpu.VMEM),
        scratch_shapes=[
            pltpu.VMEM((2 * rows, feat), slab.dtype),
            pltpu.VMEM((GROUPS, width, feat), landmarks.dtype),
            pltpu.VMEM((GROUPS, HALVES, n_ritz, block), jnp.bfloat16),
            pltpu.VMEM((n_ritz, 2 * rows), jnp.float32),
            pltpu.VMEM((n_ritz, rows), jnp.float32),
            pltpu.VMEM((n_ritz, rows), jnp.float32),
            pltpu.VMEM((n_lm, n_ritz, chunk), jnp.float32),
            pltpu.VMEM((n_lm, n_ritz, chunk), wire),
            pltpu.VMEM((n_lm - 1, n_ritz, chunk), wire),
            pltpu.VMEM((n_lm, n_ritz, chunk), wire),
            pltpu.VMEM(codes.shape[::-1], codes.dtype),
            pltpu.SMEM(exponents.shape, exponents.dtype),
            pltpu.VMEM(eigvec.shape[::-1], eigvec.dtype),
            pltpu.VMEM((1, n_ritz), ritz.dtype),
            dma((6,)),
            dma((2,)),
            dma((3 * QUARTERS,)),
            dma((16,)),
            dma((14,)),
            dma((GROUPS, QUARTERS)),
            dma((GROUPS, HALVES)),
            dma((2,)),
            dma((n_lm - 1,)),
            dma,
            dma((n_lm - 1,)),
            dma((n_lm - 1,)),
            pltpu.SemaphoreType.REGULAR((3,)),
        ],
        compiler_params=pltpu.CompilerParams(collective_id=0, has_side_effects=True, vmem_limit_bytes=56 * 2**20),
        name="nystrom",
    )(slab, landmarks, codes.T, exponents, eigvec.T, ritz.reshape(1, n_ritz))
    return extended.T


def solution(mesh):
    return jax.shard_map(
        local,
        mesh=mesh,
        in_specs=(
            P("sl", None),
            P(("lm", "sl"), None),
            P(("lm", "sl"), None),
            P(("lm", "sl")),
            P(),
            P(),
        ),
        out_specs=P("sl", None),
        check_vma=False,
    )
```

time: 57.7 us -> 48 us (0.83)
  Pallas kernels: 55.1 us -> 45.9 us
  other arithmetic: 2.4 us -> 0 us
  local copies, waits for them, and re-layouts: 0 us -> 1.67 us
    pallas_call x1, Pallas kernels: 55.1 us -> 45.9 us  [local(): pl.pallas_call(kernel, out_shape=jax.ShapeDtypeStruct((n_ritz, rows), jnp...]
    transpose x1 -> x0, other arithmetic: 1.74 us -> none  [local(): return (summed * factor[:, None]).T]
    unnamed x0 -> x1, local copies, waits for them, and re-layouts: none -> 1.67 us
    div x1 -> x0, other arithmetic: 0.66 us -> none  [local(): factor = 1.0 / (ritz * math.sqrt(total_land))]
where the time goes in v3:
time: 48 us; the launch traced here: 47.6 us
  Pallas kernels  45.9 us (96%)
  local copies, waits for them, and re-layouts  1.67 us (3%)
    pallas_call x1, Pallas kernels, local(): pl.pallas_call(kernel, out_shape=jax.ShapeDtypeStruct((n_ritz, rows), jnp...  45.9 us
    unnamed x1, local copies, waits for them, and re-layouts  1.67 us

profile of v3, /device:TPU:0, one launch (start us, length us, event | category | flops | bytes accessed | tf_op | source)
XLA Modules:
  0.0 47.6 jit_solution(15403857258088169630)
XLA Ops:
  0.0 45.9 %nystrom.1 = f32[64,1024]{1,0:T(8,128)} custom-call(bf16[1024,1024]{1,0:T(8,128)(2,1)} %slab_hbm.1, bf16[256,1024]{1,0:T(8,128)(2,1)} %land_hbm.1, bf16[96,256]{1,0:T(8,128)(2,1)} %bitcast.5, s32[2]{0:T(128)} %exponents_hbm.1, bf16[64,96]{1,0:T(8,128)(2,1)} %bitcast.6, f32[1,64]{1,0:T(1,128)} %bitcast.7), custom_call_target="tpu_custom_call" | custom-call | tf_op jit(solution)/shard_map/nystrom/pallas_call | solution.py:254
  45.9 1.7 %copy.8 = f32[1024,64]{0,1:T(8,128)} copy(f32[1024,64]{0,1:T(8,128)} %bitcast.4) | data formatting | bytes 524288

commit v4 on v3

--- a/solution.py
+++ b/solution.py
@@ -26,9 +26,9 @@
 
 
 def kernel(
-    slab_hbm, land_hbm, codes_hbm, exponents_hbm, eigvec_hbm, ritz_hbm, out_ref,
-    slab, land, vec, acc, swap_out, swap_in, total, rs_out, rs_in, ag_in, codes, exponents, eigvec, ritz,
-    load_sem, slab_sem, own_send, fwd_send, vec_send, land_recv, vec_recv, swap_sem, rs_send, rs_recv, ag_send, ag_recv, near,
+    slab_hbm, land_hbm, codes_hbm, exponents_hbm, eigvec_hbm, ritz_hbm, out_hbm,
+    slab, land, vec, acc, swap_out, swap_in, total, rs_out, rs_in, ag_in, out, codes, exponents, eigvec, ritz,
+    load_sem, slab_sem, own_send, fwd_send, vec_send, land_recv, vec_recv, swap_sem, rs_send, rs_recv, ag_send, ag_recv, near, out_sem,
 ):
     rows, feat = slab_hbm.shape
     width = land_hbm.shape[0]
@@ -228,18 +228,24 @@
     for r in range(n_lm - 1):
         piece = piece + rs_in[r].astype(jnp.float32)
     ag_in[lm] = (piece * factor).astype(ag_in.dtype)
-    gathered = []
+    gathered, written = {}, []
     for r in (5, 3, 4, 2, 6, 1, 7):
         copy = remote(ag_in.at[lm], ag_in.at[lm], ag_send.at[r - 1], ag_recv.at[r - 1], peer(r))
         copy.start()
-        gathered.append(copy)
-    for copy in gathered:
-        copy.wait_recv()
-    for j in range(n_lm):
-        out_ref[:, j * chunk:(j + 1) * chunk] = ag_in[j].astype(out_ref.dtype)
-
-    for copy in sent + gathered + [swap_slab, swap]:
+        gathered[r] = copy
+
+    for r in (0, 2, 6, 4, 1, 7, 3, 5):
+        if r:
+            gathered[r].wait_recv()
+        j = lax.rem(lm + n_lm - r, n_lm)
+        out[j] = ag_in[j].astype(out.dtype)
+        written.append(pltpu.make_async_copy(out.at[j], out_hbm.at[:, pl.ds(pl.multiple_of(j * chunk, chunk), chunk)], out_sem.at[r]))
+        written[-1].start()
+
+    for copy in sent + list(gathered.values()) + [swap_slab, swap]:
         copy.wait_send()
+    for copy in written:
+        copy.wait()
 
 
 def local(slab, landmarks, codes, exponents, eigvec, ritz):
@@ -255,7 +261,7 @@
         kernel,
         out_shape=jax.ShapeDtypeStruct((n_ritz, rows), jnp.float32),
         in_specs=[pl.BlockSpec(memory_space=pl.ANY)] * 6,
-        out_specs=pl.BlockSpec(memory_space=pltpu.VMEM),
+        out_specs=pl.BlockSpec(memory_space=pl.ANY),
         scratch_shapes=[
             pltpu.VMEM((2 * rows, feat), slab.dtype),
             pltpu.VMEM((GROUPS, width, feat), landmarks.dtype),
@@ -267,6 +273,7 @@
             pltpu.VMEM((n_lm, n_ritz, chunk), wire),
             pltpu.VMEM((n_lm - 1, n_ritz, chunk), wire),
             pltpu.VMEM((n_lm, n_ritz, chunk), wire),
+            pltpu.VMEM((n_lm, n_ritz, chunk), jnp.float32),
             pltpu.VMEM(codes.shape[::-1], codes.dtype),
             pltpu.SMEM(exponents.shape, exponents.dtype),
             pltpu.VMEM(eigvec.shape[::-1], eigvec.dtype),
@@ -284,6 +291,7 @@
             dma((n_lm - 1,)),
             dma((n_lm - 1,)),
             pltpu.SemaphoreType.REGULAR((3,)),
+            dma((n_lm,)),
         ],
         compiler_params=pltpu.CompilerParams(collective_id=0, has_side_effects=True, vmem_limit_bytes=56 * 2**20),
         name="nystrom",

time: 48 us -> 48 us (level)
  no operation moved by 1% of the time
where the time goes in v4:
time: 48 us; the launch traced here: 47.5 us
  Pallas kernels  45.8 us (95%)
  local copies, waits for them, and re-layouts  1.67 us (3%)
    pallas_call x1, Pallas kernels, local(): pl.pallas_call(kernel, out_shape=jax.ShapeDtypeStruct((n_ritz, rows), jnp...  45.8 us
    unnamed x1, local copies, waits for them, and re-layouts  1.67 us

profile of v4, /device:TPU:0, one launch (start us, length us, event | category | flops | bytes accessed | tf_op | source)
XLA Modules:
  0.0 47.5 jit_solution(10925132790119515267)
XLA Ops:
  0.0 45.8 %nystrom.1 = f32[64,1024]{1,0:T(8,128)} custom-call(bf16[1024,1024]{1,0:T(8,128)(2,1)} %slab_hbm.1, bf16[256,1024]{1,0:T(8,128)(2,1)} %land_hbm.1, bf16[96,256]{1,0:T(8,128)(2,1)} %bitcast.5, s32[2]{0:T(128)} %exponents_hbm.1, bf16[64,96]{1,0:T(8,128)(2,1)} %bitcast.6, f32[1,64]{1,0:T(1,128)} %bitcast.7), custom_call_target="tpu_custom_call" | custom-call | tf_op jit(solution)/shard_map/nystrom/pallas_call | solution.py:260
  45.8 1.7 %copy.8 = f32[1024,64]{0,1:T(8,128)} copy(f32[1024,64]{0,1:T(8,128)} %bitcast.4) | data formatting | bytes 524288

commit v5 on v3

--- a/solution.py
+++ b/solution.py
@@ -27,7 +27,7 @@
 
 def kernel(
     slab_hbm, land_hbm, codes_hbm, exponents_hbm, eigvec_hbm, ritz_hbm, out_ref,
-    slab, land, vec, acc, swap_out, swap_in, total, rs_out, rs_in, ag_in, codes, exponents, eigvec, ritz,
+    slab, land, vec, acc, swap_out, swap_in, rs_out, rs_in, ag_in, codes, exponents, eigvec, ritz,
     load_sem, slab_sem, own_send, fwd_send, vec_send, land_recv, vec_recv, swap_sem, rs_send, rs_recv, ag_send, ag_recv, near,
 ):
     rows, feat = slab_hbm.shape
@@ -209,22 +209,20 @@
     for q in (0, 2, 1, 3):
         arrive(7, q)
     multiply(7, 1, 1, 2)
-    swap_out[...] = acc[:, rows:]
+    swap_out[...] = acc[:, rows:].astype(swap_out.dtype)
     swap = remote(swap_out, swap_in, swap_sem.at[0], swap_sem.at[1], partner)
     swap.start()
     multiply(7, 1, 0, 1)
     pl.semaphore_wait(near.at[2], len(ring))
     swap.wait_recv()
-    for j in range(n_lm):
-        lanes = slice(j * chunk, (j + 1) * chunk)
-        piece = acc[:, lanes] + swap_in[:, lanes]
-        total[j] = piece
-        rs_out[j] = piece.astype(rs_out.dtype)
-    for r in (5, 3, 4, 2, 6, 1, 7):
+    for r in (5, 3, 4, 2, 6, 1, 7, 0):
         j = lax.rem(lm + r, n_lm)
-        start(remote(rs_out.at[j], rs_in.at[r - 1], rs_send.at[r - 1], rs_recv, peer(r)))
+        lanes = pl.ds(pl.multiple_of(j * chunk, chunk), chunk)
+        piece = acc[:, lanes] + swap_in[:, lanes].astype(jnp.float32)
+        if r:
+            rs_out[j] = piece.astype(rs_out.dtype)
+            start(remote(rs_out.at[j], rs_in.at[r - 1], rs_send.at[r - 1], rs_recv, peer(r)))
     remote(rs_in, rs_in, fwd_send.at[0], rs_recv, partner).wait_recv()
-    piece = total[lm]
     for r in range(n_lm - 1):
         piece = piece + rs_in[r].astype(jnp.float32)
     ag_in[lm] = (piece * factor).astype(ag_in.dtype)
@@ -261,9 +259,8 @@
             pltpu.VMEM((GROUPS, width, feat), landmarks.dtype),
             pltpu.VMEM((GROUPS, HALVES, n_ritz, block), jnp.bfloat16),
             pltpu.VMEM((n_ritz, 2 * rows), jnp.float32),
-            pltpu.VMEM((n_ritz, rows), jnp.float32),
-            pltpu.VMEM((n_ritz, rows), jnp.float32),
-            pltpu.VMEM((n_lm, n_ritz, chunk), jnp.float32),
+            pltpu.VMEM((n_ritz, rows), wire),
+            pltpu.VMEM((n_ritz, rows), wire),
             pltpu.VMEM((n_lm, n_ritz, chunk), wire),
             pltpu.VMEM((n_lm - 1, n_ritz, chunk), wire),
             pltpu.VMEM((n_lm, n_ritz, chunk), wire),

time: 48 us -> 47.4 us (0.987)
  no operation moved by 1% of the time
where the time goes in v5:
time: 47.4 us; the launch traced here: 47.3 us
  Pallas kernels  45.6 us (96%)
  local copies, waits for them, and re-layouts  1.67 us (4%)
    pallas_call x1, Pallas kernels, local(): pl.pallas_call(kernel, out_shape=jax.ShapeDtypeStruct((n_ritz, rows), jnp...  45.6 us
    unnamed x1, local copies, waits for them, and re-layouts  1.67 us

profile of v5, /device:TPU:0, one launch (start us, length us, event | category | flops | bytes accessed | tf_op | source)
XLA Modules:
  0.0 47.3 jit_solution(1118232498309294188)
XLA Ops:
  0.0 45.6 %nystrom.1 = f32[64,1024]{1,0:T(8,128)} custom-call(bf16[1024,1024]{1,0:T(8,128)(2,1)} %slab_hbm.1, bf16[256,1024]{1,0:T(8,128)(2,1)} %land_hbm.1, bf16[96,256]{1,0:T(8,128)(2,1)} %bitcast.5, s32[2]{0:T(128)} %exponents_hbm.1, bf16[64,96]{1,0:T(8,128)(2,1)} %bitcast.6, f32[1,64]{1,0:T(1,128)} %bitcast.7), custom_call_target="tpu_custom_call" | custom-call | tf_op jit(solution)/shard_map/nystrom/pallas_call | solution.py:252
  45.6 1.7 %copy.8 = f32[1024,64]{0,1:T(8,128)} copy(f32[1024,64]{0,1:T(8,128)} %bitcast.4) | data formatting | bytes 524288

commit v6 on v5

--- a/solution.py
+++ b/solution.py
@@ -27,7 +27,7 @@
 
 def kernel(
     slab_hbm, land_hbm, codes_hbm, exponents_hbm, eigvec_hbm, ritz_hbm, out_ref,
-    slab, land, vec, acc, swap_out, swap_in, rs_out, rs_in, ag_in, codes, exponents, eigvec, ritz,
+    slab, land, vec, acc, swap_out, swap_in, own_sums, rs_out, rs_in, ag_in, codes, exponents, eigvec, ritz,
     load_sem, slab_sem, own_send, fwd_send, vec_send, land_recv, vec_recv, swap_sem, rs_send, rs_recv, ag_send, ag_recv, near,
 ):
     rows, feat = slab_hbm.shape
@@ -208,20 +208,38 @@
         arrive_vec(7, half)
     for q in (0, 2, 1, 3):
         arrive(7, q)
-    multiply(7, 1, 1, 2)
-    swap_out[...] = acc[:, rows:].astype(swap_out.dtype)
-    swap = remote(swap_out, swap_in, swap_sem.at[0], swap_sem.at[1], partner)
-    swap.start()
-    multiply(7, 1, 0, 1)
-    pl.semaphore_wait(near.at[2], len(ring))
-    swap.wait_recv()
-    for r in (5, 3, 4, 2, 6, 1, 7, 0):
-        j = lax.rem(lm + r, n_lm)
-        lanes = pl.ds(pl.multiple_of(j * chunk, chunk), chunk)
-        piece = acc[:, lanes] + swap_in[:, lanes].astype(jnp.float32)
-        if r:
-            rs_out[j] = piece.astype(rs_out.dtype)
-            start(remote(rs_out.at[j], rs_in.at[r - 1], rs_send.at[r - 1], rs_recv, peer(r)))
+    part = n_lm // 2
+    mine = (lm // part) * part
+    other = part - mine
+
+    def multiply_last(side_at, first_chunk):
+        at = pl.ds(pl.multiple_of(side_at * rows + first_chunk * chunk, part * chunk), part * chunk)
+        scores = lax.dot_general(land[7], slab[at], NT, preferred_element_type=jnp.float32)
+        affinity = jnp.exp2(scores * scale).astype(jnp.bfloat16)
+        coeffs = jnp.concatenate([vec[7, half] for half in range(HALVES)], axis=1)
+        return acc[:, at] + lax.dot_general(coeffs, affinity, NN, preferred_element_type=jnp.float32)
+
+    swaps = []
+    for k, first_chunk in enumerate((other, mine)):
+        swap_out[k] = multiply_last(1, first_chunk).astype(swap_out.dtype)
+        swaps.append(remote(swap_out.at[k], swap_in.at[k], swap_sem.at[k], swap_sem.at[2 + k], partner))
+        swaps[k].start()
+    for k, first_chunk in enumerate((other, mine)):
+        sums = multiply_last(0, first_chunk)
+        if k == 0:
+            pl.semaphore_wait(near.at[2], len(ring))
+        swaps[k].wait_recv()
+        sums = sums + swap_in[k].astype(jnp.float32)
+        if k == 1:
+            own_sums[...] = jnp.stack([sums[:, n * chunk:(n + 1) * chunk] for n in range(part)])
+        for n in range(part):
+            j = first_chunk + n
+            rs_out[j] = sums[:, n * chunk:(n + 1) * chunk].astype(rs_out.dtype)
+        for n in range(k, part):
+            j = first_chunk + lax.rem(lm + (3, 2, 1, 0)[n] if k == 0 else lm + n, part)
+            d = lax.rem(j - lm + n_lm, n_lm)
+            start(remote(rs_out.at[j], rs_in.at[d - 1], rs_send.at[d - 1], rs_recv, (j, sl)))
+    piece = own_sums[lax.rem(lm, part)]
     remote(rs_in, rs_in, fwd_send.at[0], rs_recv, partner).wait_recv()
     for r in range(n_lm - 1):
         piece = piece + rs_in[r].astype(jnp.float32)
@@ -236,7 +254,7 @@
     for j in range(n_lm):
         out_ref[:, j * chunk:(j + 1) * chunk] = ag_in[j].astype(out_ref.dtype)
 
-    for copy in sent + gathered + [swap_slab, swap]:
+    for copy in sent + gathered + swaps + [swap_slab]:
         copy.wait_send()
 
 
@@ -259,8 +277,9 @@
             pltpu.VMEM((GROUPS, width, feat), landmarks.dtype),
             pltpu.VMEM((GROUPS, HALVES, n_ritz, block), jnp.bfloat16),
             pltpu.VMEM((n_ritz, 2 * rows), jnp.float32),
-            pltpu.VMEM((n_ritz, rows), wire),
-            pltpu.VMEM((n_ritz, rows), wire),
+            pltpu.VMEM((HALVES, n_ritz, rows // 2), wire),
+            pltpu.VMEM((HALVES, n_ritz, rows // 2), wire),
+            pltpu.VMEM((n_lm // 2, n_ritz, chunk), jnp.float32),
             pltpu.VMEM((n_lm, n_ritz, chunk), wire),
             pltpu.VMEM((n_lm - 1, n_ritz, chunk), wire),
             pltpu.VMEM((n_lm, n_ritz, chunk), wire),
@@ -275,7 +294,7 @@
             dma((14,)),
             dma((GROUPS, QUARTERS)),
             dma((GROUPS, HALVES)),
-            dma((2,)),
+            dma((4,)),
             dma((n_lm - 1,)),
             dma,
             dma((n_lm - 1,)),

time: 47.4 us -> 47.2 us (level)
  no operation moved by 1% of the time
where the time goes in v6:
time: 47.2 us; the launch traced here: 47.1 us
  Pallas kernels  45.4 us (96%)
  local copies, waits for them, and re-layouts  1.67 us (4%)
    pallas_call x1, Pallas kernels, local(): pl.pallas_call(kernel, out_shape=jax.ShapeDtypeStruct((n_ritz, rows), jnp...  45.4 us
    unnamed x1, local copies, waits for them, and re-layouts  1.67 us

profile of v6, /device:TPU:0, one launch (start us, length us, event | category | flops | bytes accessed | tf_op | source)
XLA Modules:
  0.0 47.1 jit_solution(3986410969097512944)
XLA Ops:
  0.0 45.4 %nystrom.1 = f32[64,1024]{1,0:T(8,128)} custom-call(bf16[1024,1024]{1,0:T(8,128)(2,1)} %slab_hbm.1, bf16[256,1024]{1,0:T(8,128)(2,1)} %land_hbm.1, bf16[96,256]{1,0:T(8,128)(2,1)} %bitcast.5, s32[2]{0:T(128)} %exponents_hbm.1, bf16[64,96]{1,0:T(8,128)(2,1)} %bitcast.6, f32[1,64]{1,0:T(1,128)} %bitcast.7), custom_call_target="tpu_custom_call" | custom-call | tf_op jit(solution)/shard_map/nystrom/pallas_call | solution.py:270
  45.4 1.7 %copy.8 = f32[1024,64]{0,1:T(8,128)} copy(f32[1024,64]{0,1:T(8,128)} %bitcast.4) | data formatting | bytes 524288
